TPU v7x, 512 devices: a whole 4x4x16 slice. The times are simulated.
512 devices in a mesh: row: 16 (over z), col: 16 (over y, x), rep: 2 (over core).
Axes of the slice: x: 4, y: 4, z: 16, core: 2. Of those that a mesh axis runs over, the one named last changes fastest.
Arguments:
- tokens: bfloat16 [512, 4096], P(('col', 'rep'), 'row'), may hold values from -6 to 6
- grad_out: bfloat16 [512, 4096], P(('col', 'rep'), 'row'), may hold values from -2.5 to 2.5
- gate_weight: bfloat16 [4096, 14336], P('row', 'col'), may hold values from -0.09375 to 0.09375
- up_weight: bfloat16 [4096, 14336], P('row', 'col'), may hold values from -0.09375 to 0.09375
- down_weight: bfloat16 [14336, 4096], P('col', 'row'), may hold values from -0.046875 to 0.046875
- gate_keep: int32 [32, 112], P('row', 'col'), may hold values from 0 to 1, as said below
- up_keep: int32 [32, 112], P('row', 'col'), may hold values from 0 to 1, as said below
- down_keep: int32 [112, 32], P('col', 'row'), may hold values from 0 to 1, as said below
Outputs:
- mixed: bfloat16 [512, 4096], P(('col', 'rep'), 'row')
- input_grad: bfloat16 [512, 4096], P(('col', 'rep'), 'row')
- gate_weight_grad: bfloat16 [4096, 14336], P('row', 'col')
- up_weight_grad: bfloat16 [4096, 14336], P('row', 'col')
- down_weight_grad: bfloat16 [14336, 4096], P('col', 'row')
Inputs may be any that keep to these rules, and one draw needn't show every extreme that they name: `gate_keep`: 1 keeps the 128 x 128 block of the gate projection, 0 prunes it; the kept share differs from one device's region to the next. `up_keep`: 1 keeps the 128 x 128 block of the up projection, 0 prunes it; the kept share differs from one device's region to the next. `down_keep`: 1 keeps the 128 x 128 block of the down projection, 0 prunes it; the kept share differs from one device's region to the next.
All inputs are finite; a program needn't handle non-finite values.
Results may differ from a plain program's by a relative error of at most 0.025.
Values may be sent and summed in bfloat16 or wider, within the bound.
No kernel may reach another device: no remote copies, remote signals or barrier semaphores. Data moves between devices by JAX's collectives and lax.ppermute only.
A program may use at most 64 MiB of HBM per device.

v0:
```python
import jax
import jax.numpy as jnp
from jax import lax
from jax.sharding import PartitionSpec as P

PLAIN = (((1,), (0,)), ((), ()))
FLIPPED = (((1,), (1,)), ((), ()))
OVER_ROWS = (((0,), (0,)), ((), ()))


def masked(weight, keep):
    rows, cols = keep.shape
    tiled = weight.reshape(rows, weight.shape[0] // rows, cols, weight.shape[1] // cols)
    return (tiled * keep[:, None, :, None].astype(weight.dtype)).reshape(weight.shape)


def product(left, weight, flipped):
    return lax.dot_general(
        left, weight, FLIPPED if flipped else PLAIN, preferred_element_type=jnp.float32
    )


def swiglu_grads(back, gate_value, gate_sig, up_value):
    gate_grad = (back * up_value * gate_sig * (1.0 + gate_value * (1.0 - gate_sig))).astype(
        jnp.bfloat16
    )
    up_grad = (back * gate_value * gate_sig).astype(jnp.bfloat16)
    return (gate_grad, up_grad)


def per_device(
    tokens, grad_out, gate_weight, up_weight, down_weight, gate_keep, up_keep, down_keep
):
    model_block = tokens.shape[1]
    gate_used = masked(gate_weight, gate_keep)
    up_used = masked(up_weight, up_keep)
    down_used = masked(down_weight, down_keep)
    token_panel, grad_panel = (
        lax.all_gather(tokens, "col", axis=0, tiled=True),
        lax.all_gather(grad_out, "col", axis=0, tiled=True),
    )
    gate_part = product(token_panel, gate_used, False)
    up_part = product(token_panel, up_used, False)
    gate_sum, up_sum = (
        lax.psum(gate_part.astype(jnp.bfloat16), "row").astype(jnp.float32),
        lax.psum(up_part.astype(jnp.bfloat16), "row").astype(jnp.float32),
    )
    gate_sig = jax.nn.sigmoid(gate_sum)
    hidden = (gate_sum * gate_sig * up_sum).astype(jnp.bfloat16)
    back_part = product(grad_panel, down_used, True)
    back_sum = lax.psum(back_part.astype(jnp.bfloat16), "row").astype(jnp.float32)
    gate_grad, up_grad = swiglu_grads(back_sum, gate_sum, gate_sig, up_sum)
    gate_term = masked(
        lax.dot_general(token_panel, gate_grad, OVER_ROWS, preferred_element_type=jnp.float32),
        gate_keep,
    )
    up_term = masked(
        lax.dot_general(token_panel, up_grad, OVER_ROWS, preferred_element_type=jnp.float32),
        up_keep,
    )
    down_term = masked(
        lax.dot_general(hidden, grad_panel, OVER_ROWS, preferred_element_type=jnp.float32),
        down_keep,
    )
    gate_total, up_total, down_total = (
        lax.psum(gate_term.astype(jnp.bfloat16), "rep").astype(jnp.float32),
        lax.psum(up_term.astype(jnp.bfloat16), "rep").astype(jnp.float32),
        lax.psum(down_term.astype(jnp.bfloat16), "rep").astype(jnp.float32),
    )
    forward = product(hidden, down_used, False)
    backward = product(gate_grad, gate_used, True) + product(up_grad, up_used, True)
    combined = lax.psum_scatter(
        jnp.concatenate([forward, backward], axis=1).astype(jnp.bfloat16),
        "col",
        scatter_dimension=0,
        tiled=True,
    ).astype(jnp.float32)
    mixed = combined[:, :model_block].astype(jnp.bfloat16)
    input_grad = combined[:, model_block:].astype(jnp.bfloat16)
    return (
        mixed,
        input_grad,
        gate_total.astype(jnp.bfloat16),
        up_total.astype(jnp.bfloat16),
        down_total.astype(jnp.bfloat16),
    )


def solution(mesh):
    return jax.shard_map(
        per_device,
        mesh=mesh,
        in_specs=(
            P(("col", "rep"), "row"),
            P(("col", "rep"), "row"),
            P("row", "col"),
            P("row", "col"),
            P("col", "row"),
            P("row", "col"),
            P("row", "col"),
            P("col", "row"),
        ),
        out_specs=(
            P(("col", "rep"), "row"),
            P(("col", "rep"), "row"),
            P("row", "col"),
            P("row", "col"),
            P("col", "row"),
        ),
        check_vma=False,
    )
```

profile of v0, /device:TPU:1, one launch (start us, length us, event | category | flops | bytes accessed | tf_op | source)
XLA Modules:
  0.0 352.1 jit_solution(348218787414217468)
XLA Ops:
  7.2 0.0 all-reduce.5.cloned.1.call-start
  7.2 19.6 %all_gather.6 = bf16[256,256]{1,0:T(8,128)(2,1)S(1)} all-gather(bf16[16,256]{1,0:T(8,128)(2,1)} %param.8), channel_id=1, replica_groups=mesh['row'=16,'col'=16,'rep'=2] {'col'}, dimensions={0}, use_global_device_ids=true | all-gather | bytes 139264 | tf_op jit(solution)/shard_map/all_gather | solution.py:39
  26.9 0.0 copy-start.4
  26.9 1.3 copy.36
  28.2 0.1 copy.35
  28.3 17.7 %all_gather.7 = bf16[256,256]{1,0:T(8,128)(2,1)S(1)} all-gather(bf16[16,256]{1,0:T(8,128)(2,1)S(1)} %copy-done.8), channel_id=1, replica_groups=mesh['row'=16,'col'=16,'rep'=2] {'col'}, dimensions={0}, use_global_device_ids=true | all-gather | bytes 139264 | tf_op jit(solution)/shard_map/all_gather | solution.py:40
  46.0 0.1 copy.37
  46.1 0.2 copy.34
  46.4 0.5 copy-done.11
  46.8 0.1 copy.33
  46.9 0.3 mul.94
  47.2 1.1 fusion.6
  48.3 0.3 mul.90
  48.7 1.1 fusion.5
  49.7 0.3 mul.98
  50.0 0.7 copy-done.7
  50.8 1.1 fusion.7
  51.9 0.0 all-reduce.5.cloned.1.call-update
  51.9 0.0 reduce-scatter.4.cloned.1.call-start
  51.9 0.1 copy.38
  52.0 0.1 copy.39
  52.1 0.1 copy.40
  52.2 144.1 %all-reduce.5.cloned.1.call-done = (bf16[256,896]{0,1:T(8,128)(2,1)}, bf16[256,896]{0,1:T(8,128)(2,1)}, bf16[256,896]{0,1:T(8,128)(2,1)}) async-done(((bf16[256,896]{0,1:T(8,128)(2,1)}, bf16[256,896]{0,1:T(8,128)(2,1)}, bf16[256,896]{0,1:T(8,128)(2,1)}), (bf16[256,896]{0,1:T(8,128)(2,1)}, bf16[256,896]{0,1:T(8,128)(2,1)}, bf16[256,896]{0,1:T(8,128)(2,1)})) %all-reduce.5.cloned.1.call-update) | async-done | bytes 1376272 | tf_op jit(solution)/shard_map/psum | solution.py:46
  196.3 2.0 convolution_convert_fusion.3
  198.3 0.0 copy-done
  198.3 0.0 copy-done.1
  198.3 0.0 copy-done.2
  198.3 0.4 fusion.12
  198.8 0.4 fusion.19
  199.1 0.6 fusion.8
  199.8 0.8 copy.45
  200.6 0.0 reduce-scatter.4.cloned.1.call-update
  200.6 0.0 all-reduce.7.cloned.1.call-start
  200.7 0.3 mul.110
  201.0 0.7 copy-done.3
  201.6 1.2 fusion.3
  202.8 0.3 mul.107
  203.1 1.1 fusion.4
  204.2 0.3 mul.113
  204.5 1.2 fusion.2
  205.7 0.0 all-reduce.7.cloned.1.call-update
  205.7 88.4 %reduce-scatter.4.cloned.1.call-done = bf16[16,512]{1,0:T(8,128)(2,1)} async-done(((bf16[256,512]{1,0:T(8,128)(2,1)}), bf16[16,512]{1,0:T(8,128)(2,1)}) %reduce-scatter.4.cloned.1.call-update) | async-done | bytes 16400
  294.1 1.3 fusion.24
  295.5 46.3 %all-reduce.7.cloned.1.call-done = (bf16[256,896]{0,1:T(8,128)(2,1)}, bf16[256,896]{0,1:T(8,128)(2,1)}, bf16[896,256]{1,0:T(8,128)(2,1)}) async-done(((bf16[256,896]{0,1:T(8,128)(2,1)}, bf16[256,896]{0,1:T(8,128)(2,1)}, bf16[896,256]{1,0:T(8,128)(2,1)}), (bf16[256,896]{0,1:T(8,128)(2,1)}, bf16[256,896]{0,1:T(8,128)(2,1)}, bf16[896,256]{1,0:T(8,128)(2,1)})) %all-reduce.7.cloned.1.call-update) | async-done | bytes 1376272 | tf_op jit(solution)/shard_map/psum | solution.py:66
  341.8 2.0 copy.43
  343.8 1.0 copy.44
  344.8 0.0 copy-done.5
  344.8 0.8 copy.73
  (20 shorter events, 0.1 us)
Async XLA Ops:
  7.2 189.1 %all-reduce.5.cloned.1.call-start = ((), (), s32[]{:S(2)}) async-start(), calls=%async_computation.2 | async-start | bytes 2752512 | tf_op jit(solution)/shard_map/psum | solution.py:46
  26.8 1.3 copy-start.9
  26.9 1.4 copy-start.8
  26.9 19.3 %copy-start.4 = (bf16[256,896]{1,0:T(8,128)(2,1)S(1)}, bf16[256,896]{1,0:T(8,128)(2,1)}, u32[]{:S(2)}) copy-start(bf16[256,896]{1,0:T(8,128)(2,1)} %param.10) | copy-start | bytes 1376260
  28.3 17.7 %copy-start.10 = (s32[7,2]{0,1:T(2,128)S(1)}, s32[7,2]{0,1:T(2,128)}, u32[]{:S(2)}) copy-start(s32[7,2]{0,1:T(2,128)} %param.15) | copy-start | bytes 172
  46.1 0.7 copy-start.11
  49.7 1.0 copy-start.7
  51.9 242.3 %reduce-scatter.4.cloned.1.call-start = ((), (), s32[]{:S(2)}) async-start(), calls=%async_computation.1 | async-start | bytes 278528
  196.3 2.0 copy-start
  196.3 2.0 copy-start.1
  196.3 2.0 copy-start.2
  200.6 1.0 copy-start.3
  200.6 141.1 %all-reduce.7.cloned.1.call-start = ((), (), s32[]{:S(2)}) async-start(), calls=%async_computation.3 | async-start | bytes 2752512 | tf_op jit(solution)/shard_map/psum | solution.py:66
  341.8 2.0 copy-start.6
  343.8 1.0 copy-start.5
Sparse Core Ops, SparseCore 0:
  52.0 144.2 all-reduce.4
  200.7 93.3 reduce-scatter.3
  297.8 43.9 all-reduce.6
where the time goes:
time: 353 us; the launch traced here: 352 us
  waiting for transfers between devices  279 us (79%)
  blocking collectives  37.4 us (11%)
  between operations  13.9 us (4%)
  local copies, waits for them, and re-layouts  11.7 us (3%)
  matrix products  9.67 us (3%)
    psum x1, waiting for transfers between devices, per_device(): lax.psum(up_part.astype(jnp.bfloat16), 'row').astype(jnp.float32)  144 us
    unnamed x4, waiting for transfers between devices  88.5 us
    psum x1, waiting for transfers between devices, per_device(): lax.psum(gate_term.astype(jnp.bfloat16), 'rep').astype(jnp.float32)  46.3 us
    all_gather x1, blocking collectives, per_device(): lax.all_gather(tokens, 'col', axis=0, tiled=True)  19.6 us
    all_gather x1, blocking collectives, per_device(): lax.all_gather(grad_out, 'col', axis=0, tiled=True)  17.7 us
    unnamed x30, local copies, waits for them, and re-layouts  8.01 us
  transfers between devices with their start and end apart: 3, of which 3 were waited for; matrix products, arithmetic and copies ran while one was open for 2% of the time, Pallas kernels for 0%

commit v1 on v0

--- a/solution.py
+++ b/solution.py
@@ -37,7 +37,9 @@
     down_used = masked(down_weight, down_keep)
     token_panel, grad_panel = (
         lax.all_gather(tokens, "col", axis=0, tiled=True),
-        lax.all_gather(grad_out, "col", axis=0, tiled=True),
+        jnp.concatenate(
+            lax.all_to_all(jnp.stack([grad_out] * lax.axis_size("col")), "col", 0, 0), axis=0
+        ),
     )
     gate_part = product(token_panel, gate_used, False)
     up_part = product(token_panel, up_used, False)

time: 353 us -> 339 us (0.960)
  blocking collectives: 37.4 us -> 19.1 us
  starting transfers between devices: 0.12 us -> 7.7 us
  waiting for transfers between devices: 279 us -> 274 us
    all_gather x1 -> x0, blocking collectives: 17.7 us -> none  [per_device(): lax.all_gather(grad_out, 'col', axis=0, tiled=True)]
    all_to_all x0 -> x1, starting transfers between devices: none -> 7.57 us  [per_device(): lax.all_to_all(jnp.stack([grad_out] * lax.axis_size('col')), 'col', 0, 0)]
    psum x1, waiting for transfers between devices: 144 us -> 139 us  [per_device(): lax.psum(up_part.astype(jnp.bfloat16), 'row').astype(jnp.float32)]
    unnamed x30 -> x33, local copies, waits for them, and re-layouts: 8.01 us -> 9.75 us
  transfers between devices with their start and end apart: 3 -> 4, of which waited for: 3 -> 3; matrix products, arithmetic and copies ran while one was open for 2% -> 3% of each run, Pallas kernels for 0% -> 0%
where the time goes in v1:
time: 339 us; the launch traced here: 338 us
  waiting for transfers between devices  274 us (81%)
  blocking collectives  19.1 us (6%)
  local copies, waits for them, and re-layouts  15.2 us (4%)
  between operations  13.9 us (4%)
  starting transfers between devices  7.7 us (2%)
  matrix products  7.15 us (2%)
    psum x1, waiting for transfers between devices, per_device(): lax.psum(up_part.astype(jnp.bfloat16), 'row').astype(jnp.float32)  139 us
    unnamed x4, waiting for transfers between devices  88.1 us
    psum x1, waiting for transfers between devices, per_device(): lax.psum(gate_term.astype(jnp.bfloat16), 'rep').astype(jnp.float32)  46.3 us
    all_gather x1, blocking collectives, per_device(): lax.all_gather(tokens, 'col', axis=0, tiled=True)  19.1 us
    unnamed x33, local copies, waits for them, and re-layouts  9.75 us
    all_to_all x1, starting transfers between devices, per_device(): lax.all_to_all(jnp.stack([grad_out] * lax.axis_size('col')), 'col', 0, 0)  7.57 us
  transfers between devices with their start and end apart: 4, of which 3 were waited for; matrix products, arithmetic and copies ran while one was open for 3% of the time, Pallas kernels for 0%

profile of v1, /device:TPU:1, one launch (start us, length us, event | category | flops | bytes accessed | tf_op | source)
XLA Modules:
  0.0 338.4 jit_solution(14850863060494846317)
XLA Ops:
  7.2 1.4 stack.2
  8.6 7.6 %all-to-all-start = ((bf16[16,16,256]{2,1,0:T(8,128)(2,1)}), bf16[16,16,256]{2,1,0:T(8,128)(2,1)S(1)}, u32[]{:S(2)}, u32[]{:S(2)}) async-start(bf16[16,16,256]{2,1,0:T(8,128)(2,1)} %stack.2), calls=%async_computation | async-start | bytes 262144 | tf_op jit(solution)/shard_map/all_to_all | solution.py:41
  16.2 19.1 %all_gather.3 = bf16[256,256]{1,0:T(8,128)(2,1)S(1)} all-gather(bf16[16,256]{1,0:T(8,128)(2,1)} %param.8), channel_id=1, replica_groups=mesh['row'=16,'col'=16,'rep'=2] {'col'}, dimensions={0}, use_global_device_ids=true | all-gather | bytes 139264 | tf_op jit(solution)/shard_map/all_gather | solution.py:39
  35.4 0.2 copy.39
  35.6 0.4 copy-done.10
  36.0 0.1 copy.38
  36.2 0.2 copy-done.1
  36.4 0.2 copy.37
  36.6 0.5 copy-done.11
  37.1 0.1 copy.36
  37.2 0.3 mul.91
  37.5 1.1 fusion.6
  38.6 0.3 mul.87
  38.9 1.1 fusion.5
  40.0 0.1 copy.40
  40.1 0.3 mul.95
  40.5 0.6 copy-done.4
  41.0 1.1 fusion.7
  42.2 0.0 reduce-scatter.4.cloned.1.call-start
  42.2 0.1 copy.41
  42.3 0.1 copy.42
  42.4 0.1 copy.44
  42.5 0.1 copy.43
  42.6 139.1 %all-reduce.5.cloned.1.call-done = (bf16[256,896]{0,1:T(8,128)(2,1)}, bf16[256,896]{0,1:T(8,128)(2,1)}, bf16[256,896]{0,1:T(8,128)(2,1)}) async-done(((bf16[256,896]{0,1:T(8,128)(2,1)}, bf16[256,896]{0,1:T(8,128)(2,1)}, bf16[256,896]{0,1:T(8,128)(2,1)}), (bf16[256,896]{0,1:T(8,128)(2,1)}, bf16[256,896]{0,1:T(8,128)(2,1)}, bf16[256,896]{0,1:T(8,128)(2,1)})) %all-reduce.5.cloned.1.call-update) | async-done | bytes 1376272 | tf_op jit(solution)/shard_map/psum | solution.py:48
  181.7 1.8 fusion.9
  183.5 0.4 fusion.19
  183.8 0.6 copy-done.6
  184.5 0.1 copy-done.8
  184.6 0.6 fusion.8
  185.2 0.4 copy-done.5
  185.6 0.4 convolution_convert_fusion.3
  186.0 0.9 copy.51
  186.9 0.3 fusion.2
  187.3 0.5 copy.45
  187.8 0.8 copy.73
  188.6 0.3 mul.104
  188.9 1.1 fusion.4
  190.0 0.3 mul.107
  190.3 0.7 copy-done.7
  191.0 0.1 copy-done.9
  191.1 1.2 fusion.3
  192.3 88.1 %reduce-scatter.4.cloned.1.call-done = bf16[16,512]{1,0:T(8,128)(2,1)} async-done(((bf16[256,512]{1,0:T(8,128)(2,1)}), bf16[16,512]{1,0:T(8,128)(2,1)}) %reduce-scatter.4.cloned.1.call-update) | async-done | bytes 16400
  280.4 1.3 fusion.22
  281.7 46.3 %all-reduce.7.cloned.1.call-done = (bf16[256,896]{0,1:T(8,128)(2,1)}, bf16[256,896]{0,1:T(8,128)(2,1)}, bf16[896,256]{1,0:T(8,128)(2,1)}) async-done(((bf16[256,896]{0,1:T(8,128)(2,1)}, bf16[256,896]{0,1:T(8,128)(2,1)}, bf16[896,256]{1,0:T(8,128)(2,1)}), (bf16[256,896]{0,1:T(8,128)(2,1)}, bf16[256,896]{0,1:T(8,128)(2,1)}, bf16[896,256]{1,0:T(8,128)(2,1)})) %all-reduce.7.cloned.1.call-update) | async-done | bytes 1376272 | tf_op jit(solution)/shard_map/psum | solution.py:68
  328.0 2.0 copy.48
  330.1 1.0 copy.49
  331.1 0.0 copy-done.2
  331.1 0.8 copy.80
  (26 shorter events, 0.2 us)
Async XLA Ops:
  7.2 28.2 %copy-start = (bf16[256,896]{1,0:T(8,128)(2,1)S(1)}, bf16[256,896]{1,0:T(8,128)(2,1)}, u32[]{:S(2)}) copy-start(bf16[256,896]{1,0:T(8,128)(2,1)} %param.11) | copy-start | bytes 1376260
  8.6 31.5 %all-to-all-start = ((bf16[16,16,256]{2,1,0:T(8,128)(2,1)}), bf16[16,16,256]{2,1,0:T(8,128)(2,1)S(1)}, u32[]{:S(2)}, u32[]{:S(2)}) async-start(bf16[16,16,256]{2,1,0:T(8,128)(2,1)} %stack.2), calls=%async_computation | async-start | bytes 262144 | tf_op jit(solution)/shard_map/all_to_all | solution.py:41
  16.2 165.5 %all-reduce.5.cloned.1.call-start = ((), (), s32[]{:S(2)}) async-start(), calls=%async_computation.3 | async-start | bytes 2752512 | tf_op jit(solution)/shard_map/psum | solution.py:48
  35.4 0.7 copy-start.10
  35.4 1.0 copy-start.1
  36.4 0.7 copy-start.11
  38.9 1.1 copy-start.12
  40.0 1.0 copy-start.4
  42.2 238.3 %reduce-scatter.4.cloned.1.call-start = ((), (), s32[]{:S(2)}) async-start(), calls=%async_computation.2 | async-start | bytes 278528
  183.5 1.0 copy-start.6
  183.5 1.1 copy-start.8
  184.6 1.0 copy-start.5
  186.9 141.1 %all-reduce.7.cloned.1.call-start = ((), (), s32[]{:S(2)}) async-start(), calls=%async_computation.4 | async-start | bytes 2752512 | tf_op jit(solution)/shard_map/psum | solution.py:68
  190.0 1.0 copy-start.7
  190.0 1.2 copy-start.9
  328.0 2.0 copy-start.3
  330.1 1.0 copy-start.2
Sparse Core Ops, SparseCore 0:
  42.3 139.3 all-reduce.4
  187.0 93.3 reduce-scatter.3
  284.1 43.9 all-reduce.6
